TPU v7x, 256 devices: a whole 4x4x8 slice. The times are simulated.
256 devices in a mesh: freq: 128 (over z, y_lo, x, core), col: 2 (over y_hi).
Axes of the slice: x: 4, y: 4 (y_hi: 2, y_lo: 2; y = y_hi * 2 + y_lo), z: 8, core: 2. Of those that a mesh axis runs over, the one named last changes fastest.
Arguments:
- traces: bfloat16 [1024, 1024, 1024], P('freq', 'col'), may hold values from -6 to 6
- source_row: int32 [1024], replicated, may hold values from 0 to 1023, each once
Outputs:
- multiples: bfloat16 [2, 128, 1024, 1024], P(None, 'freq', None, 'col')
Inputs may be any that keep to these rules, and one draw needn't show every extreme that they name: `source_row`: a permutation of the 1024 acquisition rows.
All inputs are finite; a program needn't handle non-finite values.
Results may differ from a plain program's by a relative error of at most 0.0079.
Values may be sent and summed in bfloat16 or wider, within the bound.
No kernel may reach another device: no remote copies, remote signals or barrier semaphores. Data moves between devices by JAX's collectives and lax.ppermute only.
A program may use at most 64 MiB of HBM per device.

v0:
```python
import math
import jax
import jax.numpy as jnp
from jax import lax
from jax.sharding import PartitionSpec as P


def partner(value, axis, bit):
    return lax.ppermute(value, axis, [(i, i ^ 1 << bit) for i in range(lax.axis_size(axis))])


def dft_table(samples, kept):
    row_index = jnp.arange(2 * kept)
    frequency = (row_index % kept)[:, None]
    sample_index = jnp.arange(samples)[None, :]
    phase = frequency * sample_index % samples
    angle = 2.0 * math.pi / samples * phase.astype(jnp.float32)
    table = jnp.where(row_index[:, None] < kept, jnp.cos(angle), -jnp.sin(angle))
    return (table / jnp.sqrt(jnp.float32(samples))).astype(jnp.bfloat16)


def single_product(first, second):
    return jnp.einsum("fnk,fkh->fnh", first, second, preferred_element_type=jnp.float32)


def complex_product(left, right):
    real_part = single_product(left[0], right[0]) - single_product(left[1], right[1])
    imag_part = single_product(left[0], right[1]) + single_product(left[1], right[0])
    return jnp.stack([real_part, imag_part])


def ordered(own_block, other_block, is_first, concat_axis):
    upper = jnp.where(is_first, own_block, other_block)
    lower = jnp.where(is_first, other_block, own_block)
    return jnp.concatenate([upper, lower], concat_axis)


def mirror(block):
    return jnp.swapaxes(block, 2, 3)


def average(first, second):
    return ((first.astype(jnp.float32) + second.astype(jnp.float32)) * 0.5).astype(jnp.bfloat16)


def shards(traces, source_row):
    samples = traces.shape[2]
    kept = samples // 8
    table = dft_table(samples, kept)
    spectrum = jnp.einsum("kt,srt->ksr", table, traces, preferred_element_type=jnp.float32).astype(
        jnp.bfloat16
    )
    spectrum = spectrum.reshape(2, kept, traces.shape[0], traces.shape[1])
    acquired = lax.all_to_all(spectrum, "freq", split_axis=1, concat_axis=2, tiled=True)
    arranged = jnp.take(acquired, source_row, axis=2)
    width = arranged.shape[3]
    column_half = lax.axis_index("col")
    is_first = column_half == 0
    mine = lax.dynamic_slice_in_dim(arranged, column_half * width, width, 2)
    theirs = lax.dynamic_slice_in_dim(arranged, (1 - column_half) * width, width, 2)
    mirrored = partner(theirs, "col", 0)
    transposed = ordered(mirror(mine), mirror(mirrored), is_first, 2)
    spectral = average(arranged, transposed)
    whole = lax.all_gather(spectral, "col", axis=3, tiled=True)
    scale = 1.0 / math.sqrt(spectral.shape[2])
    square = (scale * complex_product(whole, spectral)).astype(jnp.bfloat16)
    cube = scale * complex_product(whole, square)
    return (spectral.astype(jnp.float32) - square.astype(jnp.float32) + cube).astype(jnp.bfloat16)


def solution(mesh):
    in_specs = (P("freq", "col", None), P())
    out_specs = P(None, "freq", None, "col")
    return jax.shard_map(shards, mesh=mesh, in_specs=in_specs, out_specs=out_specs, check_vma=False)
```

profile of v0, /device:TPU:1, one launch (start us, length us, event | category | flops | bytes accessed | tf_op | source)
XLA Modules:
  0.0 218.2 jit_solution(4405129899482517952)
XLA Ops:
  6.5 9.8 %convolution_convert_fusion = bf16[256,8,512]{2,0,1:T(8,128)(2,1)S(1)} fusion(bf16[8,512,1024]{2,1,0:T(8,128)(2,1)} %param.2, s32[256]{0:T(256)S(1)} %and_select_fusion, pred[256]{0:T(512)(128)(4,1)S(1)} %iota_compare_fusion), kind=kOutput, calls=%fused_computation.15 | convolution fusion | flops 2153250816 | bytes 10487040 | tf_op jit(solution)/shard_map/kt,srt->ksr/dot_general | solution.py:50
  16.4 2.5 %copy.8 = bf16[2,128,8,512]{3,2,0,1:T(8,128)(2,1)} copy(bf16[2,128,8,512]{3,1,0,2:T(8,128)(2,1)S(1)} %bitcast.53) | data formatting | bytes 4194304 | tf_op jit(solution)/shard_map/reshape | solution.py:53
  18.9 0.0 copy-start.2
  18.9 14.9 %all-to-all-start = ((bf16[2,128,8,512]{3,2,0,1:T(8,128)(2,1)}), bf16[2,128,8,512]{3,2,0,1:T(8,128)(2,1)S(1)}, u32[]{:S(2)}, u32[]{:S(2)}) async-start(bf16[2,128,8,512]{3,2,0,1:T(8,128)(2,1)} %copy.8), calls=%async_computation | async-start | bytes 4194304 | tf_op jit(solution)/shard_map/all_to_all | solution.py:54
  33.8 0.2 all-gather.2.cloned.1.call-start
  34.0 0.0 copy-done.2
  34.1 50.9 %all-to-all-done = bf16[2,128,8,512]{3,2,0,1:T(8,128)(2,1)S(1)} async-done(((bf16[2,128,8,512]{3,2,0,1:T(8,128)(2,1)}), bf16[2,128,8,512]{3,2,0,1:T(8,128)(2,1)S(1)}, u32[]{:S(2)}, u32[]{:S(2)}) %all-to-all-start) | async-done | bytes 2097184 | tf_op jit(solution)/shard_map/all_to_all | solution.py:54
  85.0 0.2 copy.14
  85.1 2.2 copy.10
  87.3 10.9 %gather_fusion = bf16[1024,2,512]{2,1,0:T(2,128)(2,1)} fusion(bf16[2,1024,512]{2,0,1:T(2,128)(2,1)S(1)} %copy.10, s32[1024]{0:T(1024)S(1)} %fusion.22), kind=kCustom, calls=%fused_computation | custom fusion | bytes 4198400 | tf_op jit(solution)/shard_map/jit(_take)/gather | solution.py:55
  98.2 6.2 %copy.11 = bf16[1024,2,512]{0,2,1:T(8,128)(2,1)} copy(bf16[1024,2,512]{2,1,0:T(2,128)(2,1)} %gather_fusion) | data formatting | bytes 4194304 | tf_op jit(solution)/shard_map/jit(_take)/gather | solution.py:55
  104.5 1.8 bitcast_select_fusion
  106.3 1.1 constant_dynamic-slice_fusion
  107.3 2.6 %collective-permute-start = (bf16[2,1,512,512]{2,3,1,0:T(8,128)(2,1)}, bf16[2,1,512,512]{2,3,1,0:T(8,128)(2,1)S(1)}, u32[]{:S(2)}, u32[]{:S(2)}) collective-permute-start(bf16[2,1,512,512]{2,3,1,0:T(8,128)(2,1)} %constant_dynamic-slice_fusion), channel_id=1, source_target_pairs={{0,1},{1,0},{2,3},{3,2},{4,5},{5,4},{6,7},{7,6},{8,9},{9,8},{10,11... | collective-permute-start | bytes 3145736 | tf_op jit(solution)/shard_map/ppermute | solution.py:9
  110.0 3.0 %copy.12 = f32[2,1,1024,512]{3,2,1,0:T(8,128)} copy(bf16[2,1,1024,512]{2,3,1,0:T(8,128)(2,1)S(1)} %bitcast_select_fusion) | data formatting | bytes 6291456 | tf_op jit(solution)/shard_map/convert_element_type | solution.py:43
  112.9 0.0 copy-start.1
  112.9 20.4 %collective-permute-done = bf16[2,1,512,512]{2,3,1,0:T(8,128)(2,1)S(1)} collective-permute-done((bf16[2,1,512,512]{2,3,1,0:T(8,128)(2,1)}, bf16[2,1,512,512]{2,3,1,0:T(8,128)(2,1)S(1)}, u32[]{:S(2)}, u32[]{:S(2)}) %collective-permute-start) | collective-permute-done | bytes 1048608 | tf_op jit(solution)/shard_map/ppermute | solution.py:9
  133.4 0.5 select_bitcast_fusion.1
  133.8 0.0 copy-done.1
  133.9 2.1 multiply_convert_fusion
  136.0 0.0 copy-start
  136.0 0.0 all-gather.2.cloned.1.call-update
  136.0 60.8 %all-gather.2.cloned.1.call-done = bf16[2,1,1024,1024]{3,2,1,0:T(8,128)(2,1)} async-done(((bf16[2,1,1024,512]{3,2,1,0:T(8,128)(2,1)}), bf16[2,1,1024,1024]{3,2,1,0:T(8,128)(2,1)}) %all-gather.2.cloned.1.call-update) | async-done | bytes 4194320 | tf_op jit(solution)/shard_map/all_gather | solution.py:64
  196.7 0.0 copy-done
  196.7 0.0 copy-start.3
  196.7 3.0 %fusion.5 = f32[1024,512]{1,0:T(8,128)S(1)} fusion(bf16[2,1,1024,1024]{3,2,1,0:T(8,128)(2,1)} %all-gather.2.cloned.1.call-done, bf16[2,1,1024,512]{3,2,1,0:T(8,128)(2,1)S(1)} %copy-done), kind=kOutput, calls=%fused_computation.21 | convolution fusion | flops 1073741824 | bytes 5242880 | tf_op jit(solution)/shard_map/fnk,fkh->fnh/dot_general | solution.py:23
  199.7 0.0 copy-done.3
  199.7 1.2 fusion.6
  201.0 1.2 add_bitcast_fusion.1
  202.2 1.2 subtract_bitcast_fusion.1
  203.5 0.6 fusion
  204.1 1.2 fusion.4
  205.3 1.2 fusion.3
  206.6 1.2 subtract_bitcast_fusion
  207.8 1.3 add_bitcast_fusion
  209.1 2.3 %fusion.2 = bf16[2,1,1024,512]{3,2,1,0:T(8,128)(2,1)} fusion(f32[1,1,1024,512]{3,2,1,0:T(8,128)S(1)} %add_bitcast_fusion, f32[1,1,1024,512]{3,2,1,0:T(8,128)S(1)} %subtract_bitcast_fusion, bf16[2,1,1024,512]{3,2,1,0:T(8,128)(2,1)S(1)} %copy-done, f32[1,1,1024,512]{3,2,1,0:T(8,128)S(1)} %add_bitcast_fusion.1, f32[1,1,1024,512]{3,2,1,0:T(8,128)S(1)} %subtract_bitcast_fusion.1), kind=kLoop, calls=%fused_computation.5 | loop fusion | flops 10485760 | bytes 12582912 | tf_op jit(solution)/shard_map/convert_element_type | solution.py:68
  (4 shorter events, 0.0 us)
Async XLA Ops:
  18.9 15.1 %copy-start.2 = (s32[1024]{0:T(1024)S(1)}, s32[1024]{0:T(1024)}, u32[]{:S(2)}) copy-start(s32[1024]{0:T(1024)} %param.3) | copy-start | bytes 12292
  18.9 66.1 %all-to-all-start = ((bf16[2,128,8,512]{3,2,0,1:T(8,128)(2,1)}), bf16[2,128,8,512]{3,2,0,1:T(8,128)(2,1)S(1)}, u32[]{:S(2)}, u32[]{:S(2)}) async-start(bf16[2,128,8,512]{3,2,0,1:T(8,128)(2,1)} %copy.8), calls=%async_computation | async-start | bytes 4194304 | tf_op jit(solution)/shard_map/all_to_all | solution.py:54
  33.8 163.0 %all-gather.2.cloned.1.call-start = ((), (), s32[]{:S(2)}) async-start(), calls=%async_computation.1 | async-start | bytes 6291456 | tf_op jit(solution)/shard_map/all_gather | solution.py:64
  107.3 26.0 %collective-permute-start = (bf16[2,1,512,512]{2,3,1,0:T(8,128)(2,1)}, bf16[2,1,512,512]{2,3,1,0:T(8,128)(2,1)S(1)}, u32[]{:S(2)}, u32[]{:S(2)}) collective-permute-start(bf16[2,1,512,512]{2,3,1,0:T(8,128)(2,1)} %constant_dynamic-slice_fusion), channel_id=1, source_target_pairs={{0,1},{1,0},{2,3},{3,2},{4,5},{5,4},{6,7},{7,6},{8,9},{9,8},{10,11... | collective-permute-start | bytes 3145736 | tf_op jit(solution)/shard_map/ppermute | solution.py:9
  112.9 20.9 %copy-start.1 = (f32[2,1,1024,512]{3,2,1,0:T(8,128)S(1)}, f32[2,1,1024,512]{3,2,1,0:T(8,128)}, u32[]{:S(2)}) copy-start(f32[2,1,1024,512]{3,2,1,0:T(8,128)} %copy.12) | copy-start | bytes 12582916
  136.0 60.8 %copy-start = (bf16[2,1,1024,512]{3,2,1,0:T(8,128)(2,1)S(1)}, bf16[2,1,1024,512]{3,2,1,0:T(8,128)(2,1)}, u32[]{:S(2)}) copy-start(bf16[2,1,1024,512]{3,2,1,0:T(8,128)(2,1)} %multiply_convert_fusion) | copy-start | bytes 6291460
  196.7 3.0 %copy-start.3 = (bf16[2,1,1024,1024]{3,2,1,0:T(8,128)(2,1)S(1)}, bf16[2,1,1024,1024]{3,2,1,0:T(8,128)(2,1)}, u32[]{:S(2)}) copy-start(bf16[2,1,1024,1024]{3,2,1,0:T(8,128)(2,1)} %all-gather.2.cloned.1.call-done) | copy-start | bytes 12582916
Sparse Core Ops, SparseCore 0:
  136.1 60.5 all-gather.1
where the time goes:
time: 219 us; the launch traced here: 218 us
  waiting for transfers between devices  132 us (60%)
  local copies, waits for them, and re-layouts  26 us (12%)
  matrix products  21.5 us (10%)
  starting transfers between devices  17.7 us (8%)
  between operations  13.5 us (6%)
  other arithmetic  7.23 us (3%)
    all_gather x1, waiting for transfers between devices, shards(): whole = lax.all_gather(spectral, 'col', axis=3, tiled=True)  60.8 us
    all_to_all x1, waiting for transfers between devices, shards(): lax.all_to_all(spectrum, 'freq', split_axis=1, concat_axis=2, tiled=True)  50.9 us
    ppermute x1, waiting for transfers between devices, partner(): lax.ppermute(value, axis, [(i, i ^ 1 << bit) for i in range(lax.axis_size...  20.4 us
    gather x2, local copies, waits for them, and re-layouts, shards(): arranged = jnp.take(acquired, source_row, axis=2)  17.1 us
    all_to_all x1, starting transfers between devices, shards(): lax.all_to_all(spectrum, 'freq', split_axis=1, concat_axis=2, tiled=True)  14.9 us
    dot_general x8, matrix products, single_product(): jnp.einsum('fnk,fkh->fnh', first, second, preferred_element_type=jnp.floa...  11.7 us
    dot_general x1, matrix products, shards(): jnp.einsum('kt,srt->ksr', table, traces, preferred_element_type=jnp.float32)  9.83 us
  transfers between devices with their start and end apart: 3, of which 3 were waited for; matrix products, arithmetic and copies ran while one was open for 1% of the time, Pallas kernels for 0%

commit v1 on v0

--- a/solution.py
+++ b/solution.py
@@ -51,7 +51,9 @@
         jnp.bfloat16
     )
     spectrum = spectrum.reshape(2, kept, traces.shape[0], traces.shape[1])
-    acquired = lax.all_to_all(spectrum, "freq", split_axis=1, concat_axis=2, tiled=True)
+    pieces = jnp.split(spectrum, lax.axis_size("freq"), axis=1)
+    got = lax.all_to_all(jnp.stack(pieces), "freq", 0, 0)
+    acquired = jnp.concatenate(got, axis=2)
     arranged = jnp.take(acquired, source_row, axis=2)
     width = arranged.shape[3]
     column_half = lax.axis_index("col")

time: 219 us -> 302 us (1.38)
  local copies, waits for them, and re-layouts: 26 us -> 109 us
    unnamed x8 -> x137, local copies, waits for them, and re-layouts: 0.01 us -> 79.2 us
    split x0 -> x7, local copies, waits for them, and re-layouts: none -> 4.45 us  [shards(): pieces = jnp.split(spectrum, lax.axis_size('freq'), axis=1)]
where the time goes in v1:
time: 302 us
  waiting for transfers between devices  132 us (44%)
  local copies, waits for them, and re-layouts  109 us (36%)
  matrix products  21.5 us (7%)
  starting transfers between devices  17.6 us (6%)
  between operations  13.7 us (5%)
  other arithmetic  7.23 us (2%)
    unnamed x137, local copies, waits for them, and re-layouts  79.2 us
    all_gather x1, waiting for transfers between devices, shards(): whole = lax.all_gather(spectral, 'col', axis=3, tiled=True)  60.8 us
    all_to_all x1, waiting for transfers between devices, shards(): got = lax.all_to_all(jnp.stack(pieces), 'freq', 0, 0)  51.1 us
    ppermute x1, waiting for transfers between devices, partner(): lax.ppermute(value, axis, [(i, i ^ 1 << bit) for i in range(lax.axis_size...  20.4 us
    gather x2, local copies, waits for them, and re-layouts, shards(): arranged = jnp.take(acquired, source_row, axis=2)  17.1 us
    all_to_all x1, starting transfers between devices, shards(): got = lax.all_to_all(jnp.stack(pieces), 'freq', 0, 0)  14.9 us
    dot_general x8, matrix products, single_product(): jnp.einsum('fnk,fkh->fnh', first, second, preferred_element_type=jnp.floa...  11.7 us
    dot_general x1, matrix products, shards(): jnp.einsum('kt,srt->ksr', table, traces, preferred_element_type=jnp.float32)  9.83 us
  transfers between devices with their start and end apart: 3, of which 3 were waited for; matrix products, arithmetic and copies ran while one was open for 1% of the time, Pallas kernels for 0%

profile of v1, /device:TPU:1, one launch (start us, length us, event | category | flops | bytes accessed | tf_op | source)
XLA Modules:
  0.0 301.7 jit_solution(18191914180686490493)
XLA Ops:
  6.5 9.8 %convolution_convert_fusion = bf16[256,8,512]{2,0,1:T(8,128)(2,1)S(1)} fusion(bf16[8,512,1024]{2,1,0:T(8,128)(2,1)} %param.2, s32[256]{0:T(256)S(1)} %and_select_fusion, pred[256]{0:T(512)(128)(4,1)S(1)} %iota_compare_fusion), kind=kOutput, calls=%fused_computation.14 | convolution fusion | flops 2153250816 | bytes 10487040 | tf_op jit(solution)/shard_map/kt,srt->ksr/dot_general | solution.py:50
  16.9 0.6 fusion.33
  17.5 0.7 fusion.31
  18.2 0.7 fusion.32
  18.9 0.7 fusion.29
  19.6 0.6 fusion.30
  20.2 0.7 fusion.28
  20.9 0.6 constant_dynamic-update-slice_fusion.127
  21.5 0.6 constant_dynamic-update-slice_fusion.126
  22.1 0.6 constant_dynamic-update-slice_fusion.125
  22.7 0.6 constant_dynamic-update-slice_fusion.124
  23.3 0.6 constant_dynamic-update-slice_fusion.123
  24.0 0.6 constant_dynamic-update-slice_fusion.122
  24.6 0.6 constant_dynamic-update-slice_fusion.121
  25.2 0.6 constant_dynamic-update-slice_fusion.120
  26.4 0.6 constant_dynamic-update-slice_fusion.118
  27.0 0.6 constant_dynamic-update-slice_fusion.117
  27.6 0.6 constant_dynamic-update-slice_fusion.116
  28.3 0.6 constant_dynamic-update-slice_fusion.115
  29.5 0.6 constant_dynamic-update-slice_fusion.113
  30.1 0.6 constant_dynamic-update-slice_fusion.112
  30.7 0.6 constant_dynamic-update-slice_fusion.111
  31.3 0.6 constant_dynamic-update-slice_fusion.110
  31.9 0.6 constant_dynamic-update-slice_fusion.109
  32.6 0.6 constant_dynamic-update-slice_fusion.108
  92.1 0.6 constant_dynamic-update-slice_fusion.11
  99.4 14.9 %all-to-all-start = ((bf16[128,2,1,8,512]{4,3,1,2,0:T(8,128)(2,1)}), bf16[128,2,1,8,512]{4,3,1,2,0:T(8,128)(2,1)S(1)}, u32[]{:S(2)}, u32[]{:S(2)}) async-start(bf16[128,2,1,8,512]{4,3,1,2,0:T(8,128)(2,1)} %constant_dynamic-update-slice_fusion), calls=%async_computation | async-start | bytes 4194304 | tf_op jit(solution)/shard_map/all_to_all | solution.py:55
  114.4 51.1 %all-to-all-done = bf16[128,2,1,8,512]{4,3,1,2,0:T(8,128)(2,1)S(1)} async-done(((bf16[128,2,1,8,512]{4,3,1,2,0:T(8,128)(2,1)}), bf16[128,2,1,8,512]{4,3,1,2,0:T(8,128)(2,1)S(1)}, u32[]{:S(2)}, u32[]{:S(2)}) %all-to-all-start) | async-done | bytes 2097184 | tf_op jit(solution)/shard_map/all_to_all | solution.py:55
  165.6 1.3 copy-done.2
  166.9 4.0 %copy.259 = bf16[2,1,128,8,512]{4,0,3,2,1:T(2,128)(2,1)S(1)} copy(bf16[2,1,128,8,512]{4,3,0,1,2:T(8,128)(2,1)} %bitcast.571) | data formatting | bytes 4194304 | tf_op jit(solution)/shard_map/reshape | solution.py:56
  170.9 10.9 %gather_fusion = bf16[1024,2,512]{2,1,0:T(2,128)(2,1)} fusion(bf16[2,1024,512]{2,0,1:T(2,128)(2,1)S(1)} %bitcast.570, s32[1024]{0:T(1024)S(1)} %fusion.22), kind=kCustom, calls=%fused_computation | custom fusion | bytes 4198400 | tf_op jit(solution)/shard_map/jit(_take)/gather | solution.py:57
  181.8 6.2 %copy.260 = bf16[1024,2,512]{0,2,1:T(8,128)(2,1)} copy(bf16[1024,2,512]{2,1,0:T(2,128)(2,1)} %gather_fusion) | data formatting | bytes 4194304 | tf_op jit(solution)/shard_map/jit(_take)/gather | solution.py:57
  188.0 1.8 bitcast_select_fusion
  189.8 1.1 constant_dynamic-slice_fusion
  190.9 2.6 collective-permute-start
  193.5 3.0 copy.261
  196.5 20.4 %collective-permute-done = bf16[2,1,512,512]{2,3,1,0:T(8,128)(2,1)S(1)} collective-permute-done((bf16[2,1,512,512]{2,3,1,0:T(8,128)(2,1)}, bf16[2,1,512,512]{2,3,1,0:T(8,128)(2,1)S(1)}, u32[]{:S(2)}, u32[]{:S(2)}) %collective-permute-start) | collective-permute-done | bytes 1048608 | tf_op jit(solution)/shard_map/ppermute | solution.py:9
  217.4 2.1 multiply_convert_fusion
  219.5 60.8 %all-gather.2.cloned.1.call-done = bf16[2,1,1024,1024]{3,2,1,0:T(8,128)(2,1)} async-done(((bf16[2,1,1024,512]{3,2,1,0:T(8,128)(2,1)}), bf16[2,1,1024,1024]{3,2,1,0:T(8,128)(2,1)}) %all-gather.2.cloned.1.call-update) | async-done | bytes 4194320 | tf_op jit(solution)/shard_map/all_gather | solution.py:66
  280.3 3.0 fusion.5
  283.3 1.2 fusion.6
  284.5 1.2 add_bitcast_fusion.1
  285.8 1.2 subtract_bitcast_fusion.1
  287.6 1.2 fusion.4
  288.9 1.2 fusion.3
  290.1 1.2 subtract_bitcast_fusion
  291.4 1.3 add_bitcast_fusion
  292.6 2.3 fusion.2
  (127 shorter events, 68.4 us)
Async XLA Ops:
  99.4 15.0 %copy-start.3 = (s32[1024]{0:T(1024)S(1)}, s32[1024]{0:T(1024)}, u32[]{:S(2)}) copy-start(s32[1024]{0:T(1024)} %param.3) | copy-start | bytes 12292
  99.4 66.1 %all-to-all-start = ((bf16[128,2,1,8,512]{4,3,1,2,0:T(8,128)(2,1)}), bf16[128,2,1,8,512]{4,3,1,2,0:T(8,128)(2,1)S(1)}, u32[]{:S(2)}, u32[]{:S(2)}) async-start(bf16[128,2,1,8,512]{4,3,1,2,0:T(8,128)(2,1)} %constant_dynamic-update-slice_fusion), calls=%async_computation | async-start | bytes 4194304 | tf_op jit(solution)/shard_map/all_to_all | solution.py:55
  114.4 165.9 %all-gather.2.cloned.1.call-start = ((), (), s32[]{:S(2)}) async-start(), calls=%async_computation.1 | async-start | bytes 6291456 | tf_op jit(solution)/shard_map/all_gather | solution.py:66
  165.6 1.3 copy-start.2
  190.9 26.0 %collective-permute-start = (bf16[2,1,512,512]{2,3,1,0:T(8,128)(2,1)}, bf16[2,1,512,512]{2,3,1,0:T(8,128)(2,1)S(1)}, u32[]{:S(2)}, u32[]{:S(2)}) collective-permute-start(bf16[2,1,512,512]{2,3,1,0:T(8,128)(2,1)} %constant_dynamic-slice_fusion), channel_id=1, source_target_pairs={{0,1},{1,0},{2,3},{3,2},{4,5},{5,4},{6,7},{7,6},{8,9},{9,8},{10,11... | collective-permute-start | bytes 3145736 | tf_op jit(solution)/shard_map/ppermute | solution.py:9
  196.5 20.9 %copy-start.1 = (f32[2,1,1024,512]{3,2,1,0:T(8,128)S(1)}, f32[2,1,1024,512]{3,2,1,0:T(8,128)}, u32[]{:S(2)}) copy-start(f32[2,1,1024,512]{3,2,1,0:T(8,128)} %copy.261) | copy-start | bytes 12582916
  219.5 60.8 %copy-start = (bf16[2,1,1024,512]{3,2,1,0:T(8,128)(2,1)S(1)}, bf16[2,1,1024,512]{3,2,1,0:T(8,128)(2,1)}, u32[]{:S(2)}) copy-start(bf16[2,1,1024,512]{3,2,1,0:T(8,128)(2,1)} %multiply_convert_fusion) | copy-start | bytes 6291460
  280.3 3.0 copy-start.4
Sparse Core Ops, SparseCore 0:
  219.7 60.5 all-gather.1
